TPU v7x, 32 devices: a whole 2x2x4 slice. The times are simulated.
32 devices in a mesh: mom: 2 (over x), pts: 16 (over z, y, core).
Axes of the slice: x: 2, y: 2, z: 4, core: 2. Of those that a mesh axis runs over, the one named last changes fastest.
Arguments:
- amplitudes: bfloat16 [2, 2, 1, 256, 64, 128], P(None, None, None, 'mom'), may hold values from -6 to 6
- val_orbitals: bfloat16 [2, 256, 64, 512], P(None, 'mom'), may hold values from -0.25 to 0.25
- cond_orbitals: bfloat16 [2, 256, 512, 128], P(None, 'mom', 'pts'), may hold values from -0.25 to 0.25
- screened: bfloat16 [2, 256, 512, 512], P(None, None, ('pts', 'mom')), may hold values from -12 to 12
- val_energy: float32 [256, 64], P('mom', 'pts'), may hold values from -2 to -0.5
- cond_energy: float32 [256, 128], P('mom'), may hold values from 0.5 to 2
- grid_of_slot: int32 [256], replicated, may hold values from 0 to 255, as said below
- opposite_slot: int32 [256], P('mom'), may hold values from 0 to 255, as said below
Outputs:
- applied: float32 [2, 2, 1, 256, 64, 128], P(None, None, None, 'mom', 'pts')
Inputs may be any that keep to these rules, and one draw needn't show every extreme that they name: `grid_of_slot`: a permutation of the grid indices. opposite_slot[s] is the slot whose grid index is 255 - grid_of_slot[s]; it is never s, and s and opposite_slot[s] lie in aligned blocks of 128 slots whose first slots differ by 128.
All inputs are finite; a program needn't handle non-finite values.
Results may differ from a plain program's by a relative error of at most 0.006.
Values may be sent and summed in bfloat16 or wider, within the bound.
No kernel may reach another device: no remote copies, remote signals or barrier semaphores. Data moves between devices by JAX's collectives and lax.ppermute only.
A program may use at most 256 MiB of HBM per device.

v0:
```python
import math
import jax
import jax.numpy as jnp
from jax import lax
from jax.sharding import PartitionSpec as P


def partner_2(value, axis, apart):
    mask = 2**apart
    pairs = [(source, source ^ mask) for source in range(lax.axis_size(axis))]
    return lax.ppermute(value, axis, pairs)


def complex_mix(formula, left, right, left_sign, right_sign):
    real_real = jnp.einsum(formula, left[0], right[0], preferred_element_type=jnp.float32)
    imag_imag = jnp.einsum(formula, left[1], right[1], preferred_element_type=jnp.float32)
    real_imag = jnp.einsum(formula, left[0], right[1], preferred_element_type=jnp.float32)
    imag_real = jnp.einsum(formula, left[1], right[0], preferred_element_type=jnp.float32)
    return jnp.stack(
        [
            real_real - left_sign * right_sign * imag_imag,
            right_sign * real_imag + left_sign * imag_real,
        ]
    )


def on_device(
    amplitudes,
    val_orbitals,
    cond_orbitals,
    screened,
    val_energy,
    cond_energy,
    grid_of_slot,
    opposite_slot,
):
    slots_here = opposite_slot.shape[0]
    total_slots = grid_of_slot.shape[0]
    rows_here = val_energy.shape[1]
    frequency = jnp.arange(total_slots, dtype=jnp.int32)
    phases = frequency[:, None] * grid_of_slot[None, :] % total_slots
    angles = phases.astype(jnp.float32) * (2.0 * math.pi / total_slots)
    cosine_table = jnp.cos(angles).astype(jnp.bfloat16)
    sine_table = jnp.sin(angles).astype(jnp.bfloat16)
    half_product = complex_mix("bnkvc,kuc->bnkvu", amplitudes, cond_orbitals, 1.0, 1.0).astype(
        jnp.bfloat16
    )
    pair_values = complex_mix("bnkvu,kvm->bnkum", half_product, val_orbitals, 1.0, -1.0).astype(
        jnp.bfloat16
    )
    flattened = pair_values.reshape(pair_values.shape[:4] + (-1,))
    weights = screened.reshape(2, total_slots, -1)
    inverse_count = 1.0 / total_slots
    whole_k = lax.all_to_all(flattened, "mom", split_axis=4, concat_axis=3, tiled=True)
    spec_real = jnp.einsum(
        "fs,bnsc->bnfc", cosine_table, whole_k[0], preferred_element_type=jnp.float32
    ) + jnp.einsum("fs,bnsc->bnfc", sine_table, whole_k[1], preferred_element_type=jnp.float32)
    spec_imag = jnp.einsum(
        "fs,bnsc->bnfc", cosine_table, whole_k[1], preferred_element_type=jnp.float32
    ) - jnp.einsum("fs,bnsc->bnfc", sine_table, whole_k[0], preferred_element_type=jnp.float32)
    prod_real = (weights[0] * spec_real - weights[1] * spec_imag).astype(jnp.bfloat16)
    prod_imag = (weights[0] * spec_imag + weights[1] * spec_real).astype(jnp.bfloat16)
    back_real = (
        jnp.einsum("fs,bnfc->bnsc", cosine_table, prod_real, preferred_element_type=jnp.float32)
        - jnp.einsum("fs,bnfc->bnsc", sine_table, prod_imag, preferred_element_type=jnp.float32)
    ) * inverse_count
    back_imag = (
        jnp.einsum("fs,bnfc->bnsc", cosine_table, prod_imag, preferred_element_type=jnp.float32)
        + jnp.einsum("fs,bnfc->bnsc", sine_table, prod_real, preferred_element_type=jnp.float32)
    ) * inverse_count
    field_pts = lax.all_to_all(
        jnp.stack([back_real, back_imag]).astype(jnp.bfloat16),
        "mom",
        split_axis=3,
        concat_axis=4,
        tiled=True,
    )
    field_pts = field_pts.reshape(pair_values.shape)
    weighted = complex_mix("bnkum,kvm->bnkvu", field_pts, val_orbitals, 1.0, 1.0).astype(
        jnp.bfloat16
    )
    rows_mine = lax.all_to_all(weighted, "pts", split_axis=4, concat_axis=5, tiled=True)
    band_values = complex_mix(
        "bnkvu,kuc->bnkvc",
        rows_mine,
        lax.all_gather(cond_orbitals, "pts", axis=2, tiled=True),
        1.0,
        -1.0,
    )
    top_bit = lax.axis_size("mom").bit_length() - 2
    partner = partner_2(band_values.astype(jnp.bfloat16), "mom", top_bit).astype(band_values.dtype)
    mirrored = jnp.take(partner, opposite_slot % slots_here, axis=3)
    start_row = lax.axis_index("pts") * rows_here
    own_rows = lax.dynamic_slice_in_dim(amplitudes, start_row, rows_here, 4).astype(jnp.float32)
    energy_gap = cond_energy[:, None, :] - val_energy[:, :, None]
    result_real = energy_gap * own_rows[0, 0] - band_values[0, 0] - mirrored[0, 1]
    result_imag = energy_gap * own_rows[1, 0] - band_values[1, 0] + mirrored[1, 1]
    anti_real = -energy_gap * own_rows[0, 1] + band_values[0, 1] + mirrored[0, 0]
    anti_imag = -energy_gap * own_rows[1, 1] + band_values[1, 1] - mirrored[1, 0]
    return jnp.stack([jnp.stack([result_real, anti_real]), jnp.stack([result_imag, anti_imag])])


def solution(mesh):
    in_specs = (
        P(None, None, None, "mom", None, None),
        P(None, "mom", None, None),
        P(None, "mom", "pts", None),
        P(None, None, ("pts", "mom"), None),
        P("mom", "pts"),
        P("mom", None),
        P(),
        P("mom"),
    )
    out_specs = P(None, None, None, "mom", "pts", None)
    return jax.shard_map(
        on_device, mesh=mesh, in_specs=in_specs, out_specs=out_specs, check_vma=False
    )
```

profile of v0, /device:TPU:0, one launch (start us, length us, event | category | flops | bytes accessed | tf_op | source)
XLA Modules:
  0.0 1007.6 jit_solution(14866260467784046337)
XLA Ops:
  40.7 14.0 %fusion.34 = bf16[2,1,128,32,512]{4,3,0,2,1:T(8,128)(2,1)} fusion(f32[128,2,32,512]{3,2,1,0:T(8,128)} %fusion.17, bf16[2,128,64,32]{2,3,0,1:T(8,128)(2,1)} %fusion.45, bf16[2,128,64,512]{3,2,1,0:T(8,128)(2,1)} %param.9), kind=kOutput, calls=%fused_computation.51 | convolution fusion | flops 549453824 | bytes 35651584 | tf_op jit(solution)/shard_map/bnkvu,kvm->bnkum/dot_general | solution.py:16
  54.7 16.5 %copy.203 = bf16[2,1,128,32,512]{2,0,4,3,1:T(2,128)(2,1)} copy(bf16[2,1,128,32,512]{4,3,0,2,1:T(8,128)(2,1)} %fusion.34) | data formatting | bytes 16777216 | tf_op jit(solution)/shard_map/stack | solution.py:19
  71.2 12.1 %fusion.23 = f32[128,2,32,512]{3,2,1,0:T(8,128)} fusion(bf16[2,128,64,32]{2,3,0,1:T(8,128)(2,1)S(1)} %copy-done.4, bf16[2,128,64,512]{3,2,1,0:T(8,128)(2,1)} %param.9), kind=kOutput, calls=%fused_computation.40 | convolution fusion | flops 536870912 | bytes 26214400 | tf_op jit(solution)/shard_map/bnkvu,kvm->bnkum/dot_general | solution.py:17
  83.4 12.9 %fusion.37 = bf16[2,1,128,32,512]{4,3,0,2,1:T(8,128)(2,1)} fusion(bf16[2,128,64,32]{2,3,0,1:T(8,128)(2,1)S(1)} %copy-done.2, bf16[2,128,64,512]{3,2,1,0:T(8,128)(2,1)} %param.9, f32[128,2,32,512]{3,2,1,0:T(8,128)} %fusion.23), kind=kOutput, calls=%fused_computation.52 | convolution fusion | flops 549453824 | bytes 34603008 | tf_op jit(solution)/shard_map/bnkvu,kvm->bnkum/dot_general | solution.py:18
  96.3 15.7 %copy.204 = bf16[2,1,128,32,512]{2,0,4,3,1:T(2,128)(2,1)} copy(bf16[2,1,128,32,512]{4,3,0,2,1:T(8,128)(2,1)} %fusion.37) | data formatting | bytes 16777216 | tf_op jit(solution)/shard_map/stack | solution.py:19
  112.0 26.4 %pad_maximum_fusion = bf16[2,2,1,128,16384]{3,1,2,0,4:T(2,128)(2,1)} fusion(bf16[1,2,1,128,16384]{3,1,2,0,4:T(2,128)(2,1)} %bitcast.316, bf16[1,2,1,128,16384]{3,1,2,0,4:T(2,128)(2,1)} %bitcast.315), kind=kLoop, calls=%fused_computation.3 | loop fusion | flops 8388608 | bytes 33554432 | tf_op jit(solution)/shard_map/stack | solution.py:19
  148.2 12.1 %slice_convert_fusion.1 = (f32[1,256,16,512]{3,2,1,0:T(8,128)}, f32[1,256,16,512]{3,2,1,0:T(8,128)}) fusion(bf16[2,256,16,512]{3,2,1,0:T(8,128)(2,1)} %param.11), kind=kLoop, calls=%fused_computation.61 | loop fusion | flops 4194304 | bytes 25165824 | tf_op jit(solution)/shard_map/convert_element_type | solution.py:61
  160.3 9.9 copy.202
  170.2 10.0 copy.205
  180.2 150.9 %all-to-all-done = bf16[2,2,1,128,16384]{3,1,2,0,4:T(2,128)(2,1)} async-done(((bf16[2,2,1,128,16384]{3,1,2,0,4:T(2,128)(2,1)}), bf16[2,2,1,128,16384]{3,1,2,0,4:T(2,128)(2,1)}, u32[]{:S(2)}, u32[]{:S(2)}) %all-to-all-start) | async-done | bytes 16777248 | tf_op jit(solution)/shard_map/all_to_all | solution.py:54
  331.1 28.1 %copy.246 = bf16[2,2,1,128,2,8192]{3,4,5,1,2,0:T(2,128)(2,1)S(1)} copy(bf16[2,2,1,128,2,8192]{3,1,0,5,4,2:T(2,128)(2,1)} %bitcast.38) | data formatting | bytes 33554432 | tf_op jit(solution)/shard_map/all_to_all | solution.py:54
  359.2 13.0 %fusion.133 = (bf16[1,2,1,2,128,8192]{4,3,5,1,2,0:T(2,128)(2,1)}, bf16[1,2,1,2,128,8192]{4,3,5,1,2,0:T(2,128)(2,1)}) fusion(bf16[2,2,1,2,128,8192]{4,3,5,1,2,0:T(2,128)(2,1)S(1)} %bitcast.312), kind=kLoop, calls=%fused_computation.179 | loop fusion | bytes 33554432 | tf_op jit(solution)/shard_map/slice | solution.py:57
  372.2 14.1 %reshape.539 = bf16[2,256,8192]{1,2,0:T(8,128)(2,1)} reshape(bf16[1,2,1,2,128,8192]{4,3,5,1,2,0:T(2,128)(2,1)} %get-tuple-element.15) | data formatting | bytes 16777216 | tf_op jit(solution)/shard_map/reshape.28
  386.3 14.2 %reshape.538 = bf16[2,256,8192]{1,2,0:T(8,128)(2,1)} reshape(bf16[1,2,1,2,128,8192]{4,3,5,1,2,0:T(2,128)(2,1)} %get-tuple-element.16) | data formatting | bytes 16777216 | tf_op jit(solution)/shard_map/reshape.24
  400.5 12.5 %fusion.91 = f32[2,8192,256]{2,1,0:T(8,128)} fusion(bf16[2,256,8192]{1,2,0:T(8,128)(2,1)} %reshape.539, s32[256]{0:T(256)S(1)} %copy-done.6), kind=kOutput, calls=%fused_computation.134 | convolution fusion | flops 2148466688 | bytes 25166848 | tf_op jit(solution)/shard_map/fs,bnsc->bnfc/dot_general | solution.py:58
  422.1 14.8 %convolution_subtract_fusion = f32[2,8192,256]{2,1,0:T(8,128)} fusion(f32[2,8192,256]{2,1,0:T(8,128)} %fusion.91, bf16[2,256,8192]{1,2,0:T(8,128)(2,1)S(1)} %copy-done.1, s32[256]{0:T(256)S(1)} %copy-done.6), kind=kOutput, calls=%fused_computation.23 | convolution fusion | flops 2152660992 | bytes 41944064 | tf_op jit(solution)/shard_map/fs,bnsc->bnfc/dot_general | solution.py:60
  436.9 27.2 %fusion.11 = (bf16[2,256,8192]{1,2,0:T(8,128)(2,1)}, bf16[2,256,8192]{1,2,0:T(8,128)(2,1)}) fusion(f32[2,8192,256]{2,1,0:T(8,128)} %convolution_subtract_fusion, f32[256,8192]{0,1:T(8,128)} %bitcast.311, f32[256,8192]{0,1:T(8,128)} %bitcast.310, f32[2,8192,256]{2,1,0:T(8,128)} %fusion.93, bf16[2,256,8192]{1,2,0:T(8,128)(2,1)} %reshape.539, s32[256]{0:T(256)S(1)} %copy-done.6), kind=kOutput, calls=%fused_computation.28 | convolution fusion | flops 2186215424 | bytes 75498496 | tf_op jit(solution)/shard_map/fs,bnsc->bnfc/dot_general | solution.py:57
  464.1 12.5 %fusion.89 = f32[2,8192,256]{2,1,0:T(8,128)} fusion(bf16[2,256,8192]{1,2,0:T(8,128)(2,1)} %get-tuple-element.11, s32[256]{0:T(256)S(1)} %copy-done.6), kind=kOutput, calls=%fused_computation.133 | convolution fusion | flops 2148466688 | bytes 25166848 | tf_op jit(solution)/shard_map/fs,bnfc->bnsc/dot_general | solution.py:64
  485.7 13.5 %fusion.8 = bf16[1,2,1,256,8192]{3,4,1,2,0:T(8,128)(2,1)} fusion(f32[2,8192,256]{2,1,0:T(8,128)} %fusion.89, bf16[2,256,8192]{1,2,0:T(8,128)(2,1)} %get-tuple-element.12, s32[256]{0:T(256)S(1)} %copy-done.6), kind=kOutput, calls=%fused_computation.25 | convolution fusion | flops 2161049600 | bytes 33555456 | tf_op jit(solution)/shard_map/fs,bnfc->bnsc/dot_general | solution.py:65
  499.2 11.5 %fusion.9 = bf16[1,2,1,256,8192]{3,4,1,2,0:T(8,128)(2,1)} fusion(f32[2,8192,256]{2,1,0:T(8,128)} %fusion.87, bf16[2,256,8192]{1,2,0:T(8,128)(2,1)S(1)} %bitcast.309, s32[256]{0:T(256)S(1)} %copy-done.6), kind=kOutput, calls=%fused_computation.26 | convolution fusion | flops 2161049600 | bytes 33555456 | tf_op jit(solution)/shard_map/fs,bnfc->bnsc/dot_general | solution.py:69
  510.8 13.7 %pad_maximum_fusion.1 = bf16[2,2,1,256,8192]{3,4,1,2,0:T(8,128)(2,1)} fusion(bf16[1,2,1,256,8192]{3,4,1,2,0:T(8,128)(2,1)} %fusion.9, bf16[1,2,1,256,8192]{3,4,1,2,0:T(8,128)(2,1)} %fusion.8), kind=kLoop, calls=%fused_computation.4 | loop fusion | flops 8388608 | bytes 33554432 | tf_op jit(solution)/shard_map/stack | solution.py:72
  524.5 41.2 %copy.175 = bf16[2,2,1,256,8192]{4,1,2,0,3:T(2,128)(2,1)} copy(bf16[2,2,1,256,8192]{3,4,1,2,0:T(8,128)(2,1)} %pad_maximum_fusion.1) | data formatting | bytes 33554432 | tf_op jit(solution)/shard_map/stack | solution.py:72
  565.7 200.1 %all_to_all.45 = bf16[2,2,1,256,8192]{4,1,2,0,3:T(2,128)(2,1)} all-to-all(bf16[2,2,1,256,8192]{4,1,2,0,3:T(2,128)(2,1)} %copy.175), channel_id=1, replica_groups=mesh['mom'=2,'pts'=16] {'mom'}, dimensions={3} | all-to-all | bytes 33554432 | tf_op jit(solution)/shard_map/all_to_all | solution.py:71
  765.8 30.2 %copy.245 = bf16[2,2,1,2,128,8192]{5,3,1,4,2,0:T(2,128)(2,1)S(1)} copy(bf16[2,2,1,2,128,8192]{5,1,0,4,3,2:T(2,128)(2,1)} %bitcast.314) | data formatting | bytes 33554432 | tf_op jit(solution)/shard_map/all_to_all | solution.py:71
  796.1 14.9 %fusion.132 = (bf16[1,2,1,128,2,8192]{5,4,1,3,2,0:T(2,128)(2,1)}, bf16[1,2,1,128,2,8192]{5,4,1,3,2,0:T(2,128)(2,1)}) fusion(bf16[2,2,1,128,2,8192]{5,4,1,3,2,0:T(2,128)(2,1)S(1)} %bitcast.313), kind=kLoop, calls=%fused_computation.178 | loop fusion | bytes 33554432 | tf_op jit(solution)/shard_map/slice | solution.py:15
  811.0 14.3 %reshape.542 = bf16[2,128,32,512]{3,2,0,1:T(8,128)(2,1)} reshape(bf16[1,2,1,128,2,8192]{5,4,1,3,2,0:T(2,128)(2,1)} %get-tuple-element.13) | data formatting | bytes 16777216 | tf_op jit(solution)/shard_map/reshape.50
  825.2 14.3 %reshape.543 = bf16[2,128,32,512]{3,2,0,1:T(8,128)(2,1)} reshape(bf16[1,2,1,128,2,8192]{5,4,1,3,2,0:T(2,128)(2,1)} %get-tuple-element.14) | data formatting | bytes 16777216 | tf_op jit(solution)/shard_map/reshape.54
  839.5 10.1 fusion.14
  849.6 10.1 fusion.12
  868.9 10.7 %fusion.47 = bf16[1,2,1,128,64,32]{4,5,1,3,2,0:T(8,128)(2,1)} fusion(f32[128,2,32,64]{3,2,1,0:T(8,128)} %fusion.12, bf16[2,128,32,512]{3,2,0,1:T(8,128)(2,1)} %reshape.542, bf16[2,128,64,512]{3,2,1,0:T(8,128)(2,1)} %param.9), kind=kOutput, calls=%fused_computation.69 | convolution fusion | flops 537919488 | bytes 22020096 | tf_op jit(solution)/shard_map/bnkum,kvm->bnkvu/dot_general | solution.py:17
  892.1 52.0 %all_to_all.46 = bf16[2,2,1,128,64,32]{3,5,2,1,0,4:T(8,128)(2,1)S(1)} all-to-all(bf16[2,2,1,128,64,32]{3,5,2,1,0,4:T(8,128)(2,1)S(1)} %copy.177), channel_id=1, replica_groups=mesh['mom'=2,'pts'=16] {'pts'}, dimensions={4} | all-to-all | bytes 4194304 | tf_op jit(solution)/shard_map/all_to_all | solution.py:82
  980.9 12.8 %collective-permute-done = bf16[2,2,1,128,4,128]{5,3,4,2,1,0:T(8,128)(2,1)S(1)} collective-permute-done((bf16[2,2,1,128,4,128]{5,3,4,2,1,0:T(8,128)(2,1)S(1)}, bf16[2,2,1,128,4,128]{5,3,4,2,1,0:T(8,128)(2,1)S(1)}, u32[]{:S(2)}, u32[]{:S(2)}) %collective-permute-start) | collective-permute-done | bytes 524320 | tf_op jit(solution)/shard_map/ppermute | solution.py:11
  (74 shorter events, 127.3 us)
Async XLA Ops:
  6.5 942.7 %all-gather.2.cloned.1.call-start = ((), (), s32[]{:S(2)}) async-start(), calls=%async_computation.3 | async-start | bytes 35651584 | tf_op jit(solution)/shard_map/all_gather | solution.py:86
  7.3 4.6 copy-start.3
  16.0 14.9 %slice-start = ((s8[16777216]{0:T(1024)(128)(4,1)}), s8[4194304]{0:T(1024)(128)(4,1)S(1)}, s32[]{:S(2)}) async-start(s8[16777216]{0:T(1024)(128)(4,1)} %bitcast.306), calls=%async_computation.4 | async-start | bytes 8388608
  16.0 14.9 %slice-start.1 = ((s8[16777216]{0:T(1024)(128)(4,1)}), s8[4194304]{0:T(1024)(128)(4,1)S(1)}, s32[]{:S(2)}) async-start(s8[16777216]{0:T(1024)(128)(4,1)} %bitcast.306), calls=%async_computation.5 | async-start | bytes 8388608
  20.0 10.8 %slice-start.2 = ((s8[16777216]{0:T(1024)(128)(4,1)}), s8[4194304]{0:T(1024)(128)(4,1)S(1)}, s32[]{:S(2)}) async-start(s8[16777216]{0:T(1024)(128)(4,1)} %bitcast.306), calls=%async_computation.6 | async-start | bytes 8388608
  25.5 5.4 slice-start.3
  54.7 16.5 %copy-start.4 = (bf16[2,128,64,32]{2,3,0,1:T(8,128)(2,1)S(1)}, bf16[2,128,64,32]{2,3,0,1:T(8,128)(2,1)}, u32[]{:S(2)}) copy-start(bf16[2,128,64,32]{2,3,0,1:T(8,128)(2,1)} %fusion.44) | copy-start | bytes 3145732
  71.2 12.1 %copy-start.2 = (bf16[2,128,64,32]{2,3,0,1:T(8,128)(2,1)S(1)}, bf16[2,128,64,32]{2,3,0,1:T(8,128)(2,1)}, u32[]{:S(2)}) copy-start(bf16[2,128,64,32]{2,3,0,1:T(8,128)(2,1)} %fusion.45) | copy-start | bytes 3145732
  138.4 192.7 %all-to-all-start = ((bf16[2,2,1,128,16384]{3,1,2,0,4:T(2,128)(2,1)}), bf16[2,2,1,128,16384]{3,1,2,0,4:T(2,128)(2,1)}, u32[]{:S(2)}, u32[]{:S(2)}) async-start(bf16[2,2,1,128,16384]{3,1,2,0,4:T(2,128)(2,1)} %pad_maximum_fusion), calls=%async_computation | async-start | bytes 33554432 | tf_op jit(solution)/shard_map/all_to_all | solution.py:54
  386.3 14.2 %copy-start.6 = (s32[256]{0:T(256)S(1)}, s32[256]{0:T(256)}, u32[]{:S(2)}) copy-start(s32[256]{0:T(256)} %param.14) | copy-start | bytes 3076
  400.5 12.6 %copy-start.1 = (bf16[2,256,8192]{1,2,0:T(8,128)(2,1)S(1)}, bf16[2,256,8192]{1,2,0:T(8,128)(2,1)}, u32[]{:S(2)}) copy-start(bf16[2,256,8192]{1,2,0:T(8,128)(2,1)} %reshape.538) | copy-start | bytes 25165828
  464.1 12.6 %copy-start = (bf16[2,256,8192]{1,2,0:T(8,128)(2,1)S(1)}, bf16[2,256,8192]{1,2,0:T(8,128)(2,1)}, u32[]{:S(2)}) copy-start(bf16[2,256,8192]{1,2,0:T(8,128)(2,1)} %get-tuple-element.12) | copy-start | bytes 25165828
  464.1 35.1 %slice-start.4 = ((s8[8388608]{0:T(1024)(128)(4,1)}), s8[4194304]{0:T(1024)(128)(4,1)S(1)}, s32[]{:S(2)}) async-start(s8[8388608]{0:T(1024)(128)(4,1)} %bitcast.308), calls=%async_computation.8 | async-start | bytes 8388608
  476.7 22.5 %slice-start.5 = ((s8[8388608]{0:T(1024)(128)(4,1)}), s8[4194304]{0:T(1024)(128)(4,1)S(1)}, s32[]{:S(2)}) async-start(s8[8388608]{0:T(1024)(128)(4,1)} %bitcast.308), calls=%async_computation.9 | async-start | bytes 8388608
  970.4 8.9 copy-start.8
  977.5 18.9 %copy-start.5 = (f32[128,128]{1,0:T(8,128)S(1)}, f32[128,128]{1,0:T(8,128)}, u32[]{:S(2)}) copy-start(f32[128,128]{1,0:T(8,128)} %param.13) | copy-start | bytes 196612
  977.5 18.9 %copy-start.7 = (f32[128,4]{0,1:T(4,128)S(1)}, f32[128,4]{0,1:T(4,128)}, u32[]{:S(2)}) copy-start(f32[128,4]{0,1:T(4,128)} %param.12) | copy-start | bytes 6148
  978.9 14.9 %collective-permute-start = (bf16[2,2,1,128,4,128]{5,3,4,2,1,0:T(8,128)(2,1)S(1)}, bf16[2,2,1,128,4,128]{5,3,4,2,1,0:T(8,128)(2,1)S(1)}, u32[]{:S(2)}, u32[]{:S(2)}) collective-permute-start(bf16[2,2,1,128,4,128]{5,3,4,2,1,0:T(8,128)(2,1)S(1)} %pad_maximum_fusion.4), channel_id=1, source_target_pairs={{0,16},{16,0},{1,17},{17,1},{2,18},{18,2},{3,19},{19,3},{4,20},{20... | collective-permute-start | bytes 1572872 | tf_op jit(solution)/shard_map/ppermute | solution.py:11
Sparse Core Ops, SparseCore 0:
  8.9 170.7 all-gather.1
where the time goes:
time: 1020 us; the launch traced here: 1010 us
  local copies, waits for them, and re-layouts  259 us (25%)
  blocking collectives  252 us (25%)
  matrix products  246 us (24%)
  waiting for transfers between devices  164 us (16%)
  other arithmetic  61.5 us (6%)
  between operations  13.9 us (1%)
    all_to_all x1, blocking collectives, on_device(): lax.all_to_all(jnp.stack([back_real, back_imag]).astype(jnp.bfloat16), 'm...  200 us
    all_to_all x1, waiting for transfers between devices, on_device(): lax.all_to_all(flattened, 'mom', split_axis=4, concat_axis=3, tiled=True)  151 us
    another operation x6, local copies, waits for them, and re-layouts  58.6 us
    all_to_all x1, blocking collectives, on_device(): lax.all_to_all(weighted, 'pts', split_axis=4, concat_axis=5, tiled=True)  52 us
    another operation x1, local copies, waits for them, and re-layouts, on_device(): jnp.stack([back_real, back_imag]).astype(jnp.bfloat16)  41.2 us
    another operation x3, local copies, waits for them, and re-layouts, complex_mix(): jnp.stack([real_real - left_sign * right_sign * imag_imag, right_sign * r...  40.2 us
    dot_general x4, matrix products, complex_mix(): jnp.einsum(formula, left[1], right[1], preferred_element_type=jnp.float32)  35.8 us
    dot_general x4, matrix products, complex_mix(): jnp.einsum(formula, left[1], right[0], preferred_element_type=jnp.float32)  35.4 us
  transfers between devices with their start and end apart: 3, of which 2 were waited for; matrix products, arithmetic and copies ran while one was open for 53% of the time, Pallas kernels for 0%

commit v1 on v0

--- a/solution.py
+++ b/solution.py
@@ -3,6 +3,18 @@
 import jax.numpy as jnp
 from jax import lax
 from jax.sharding import PartitionSpec as P
+
+
+def in_blocks(value, dim, size):
+    lengths = value.shape
+    blocks = value.reshape(*lengths[:dim], size, lengths[dim] // size, *lengths[dim + 1 :])
+    return jnp.moveaxis(blocks, dim, 0)
+
+
+def joined_along(parts, dim):
+    parts = jnp.moveaxis(parts, 0, dim)
+    shape = parts.shape
+    return parts.reshape(*shape[:dim], shape[dim] * shape[dim + 1], *shape[dim + 2 :])
 
 
 def partner_2(value, axis, apart):
@@ -79,7 +91,15 @@
     weighted = complex_mix("bnkum,kvm->bnkvu", field_pts, val_orbitals, 1.0, 1.0).astype(
         jnp.bfloat16
     )
-    rows_mine = lax.all_to_all(weighted, "pts", split_axis=4, concat_axis=5, tiled=True)
+    size, place = (lax.axis_size("pts"), lax.axis_index("pts"))
+    pieces = in_blocks(weighted, 4, size)
+    result = pieces
+    for step in range(1, size):
+        target, source_2 = ((place + step) % size, (place - step) % size)
+        sent = lax.dynamic_index_in_dim(pieces, target, 0)
+        received = lax.ppermute(sent, "pts", [(i, (i + step) % size) for i in range(size)])
+        result = lax.dynamic_update_slice_in_dim(result, received, source_2, axis=0)
+    rows_mine = joined_along(result, 5)
     band_values = complex_mix(
         "bnkvu,kuc->bnkvc",
         rows_mine,

time: 1020 us -> 1010 us (level)
  blocking collectives: 252 us -> 0 us
  waiting for transfers between devices: 164 us -> 370 us
  starting transfers between devices: 10.2 us -> 48.9 us
    all_to_all x2 -> x0, blocking collectives: 252 us -> none  [the longest x1 200 us: on_device(): lax.all_to_all(jnp.stack([back_real, back_imag]).astype(jnp.bfloat16), 'm...]
    all_to_all x0 -> x1, waiting for transfers between devices: none -> 181 us  [on_device(): lax.all_to_all(jnp.stack([back_real, back_imag]).astype(jnp.bfloat16), 'm...]
    ppermute x0 -> x15, starting transfers between devices: none -> 28.7 us  [on_device(): lax.ppermute(sent, 'pts', [(i, (i + step) % size) for i in range(size)])]
    ppermute x0 -> x15, waiting for transfers between devices: none -> 25.2 us  [on_device(): lax.ppermute(sent, 'pts', [(i, (i + step) % size) for i in range(size)])]
    another operation x3 -> x2, local copies, waits for them, and re-layouts: 40.2 us -> 32.2 us  [complex_mix(): jnp.stack([real_real - left_sign * right_sign * imag_imag, right_sign * r...]
    another operation x3 -> x2, other arithmetic: 31.1 us -> 26.5 us  [complex_mix(): jnp.stack([real_real - left_sign * right_sign * imag_imag, right_sign * r...]
  transfers between devices with their start and end apart: 3 -> 19, of which waited for: 2 -> 9; matrix products, arithmetic and copies ran while one was open for 53% -> 53% of each run, Pallas kernels for 0% -> 0%
where the time goes in v1:
time: 1010 us; the launch traced here: 997 us
  waiting for transfers between devices  370 us (37%)
  local copies, waits for them, and re-layouts  259 us (26%)
  matrix products  247 us (24%)
  other arithmetic  57.4 us (6%)
  starting transfers between devices  48.9 us (5%)
  between operations  14.7 us (1%)
    all_to_all x1, waiting for transfers between devices, on_device(): lax.all_to_all(jnp.stack([back_real, back_imag]).astype(jnp.bfloat16), 'm...  181 us
    all_to_all x1, waiting for transfers between devices, on_device(): lax.all_to_all(flattened, 'mom', split_axis=4, concat_axis=3, tiled=True)  151 us
    another operation x6, local copies, waits for them, and re-layouts  58.8 us
    another operation x1, local copies, waits for them, and re-layouts, on_device(): jnp.stack([back_real, back_imag]).astype(jnp.bfloat16)  41.2 us
    dot_general x4, matrix products, complex_mix(): jnp.einsum(formula, left[1], right[1], preferred_element_type=jnp.float32)  35.8 us
    dot_general x4, matrix products, complex_mix(): jnp.einsum(formula, left[1], right[0], preferred_element_type=jnp.float32)  35.6 us
    dot_general x4, matrix products, complex_mix(): jnp.einsum(formula, left[0], right[1], preferred_element_type=jnp.float32)  33.9 us
    another operation x2, local copies, waits for them, and re-layouts, complex_mix(): jnp.stack([real_real - left_sign * right_sign * imag_imag, right_sign * r...  32.2 us
  transfers between devices with their start and end apart: 19, of which 9 were waited for; matrix products, arithmetic and copies ran while one was open for 53% of the time, Pallas kernels for 0%

profile of v1, /device:TPU:0, one launch (start us, length us, event | category | flops | bytes accessed | tf_op | source)
XLA Modules:
  0.0 997.3 jit_solution(3504902925507853412)
XLA Ops:
  40.8 14.0 %fusion.34 = bf16[2,1,128,32,512]{4,3,0,2,1:T(8,128)(2,1)} fusion(f32[128,2,32,512]{3,2,1,0:T(8,128)} %fusion.17, bf16[2,128,64,32]{2,3,0,1:T(8,128)(2,1)} %fusion.45, bf16[2,128,64,512]{3,2,1,0:T(8,128)(2,1)} %param.9), kind=kOutput, calls=%fused_computation.82 | convolution fusion | flops 549453824 | bytes 35651584 | tf_op jit(solution)/shard_map/bnkvu,kvm->bnkum/dot_general | solution.py:28
  54.8 16.5 %copy.204 = bf16[2,1,128,32,512]{2,0,4,3,1:T(2,128)(2,1)} copy(bf16[2,1,128,32,512]{4,3,0,2,1:T(8,128)(2,1)} %fusion.34) | data formatting | bytes 16777216 | tf_op jit(solution)/shard_map/stack | solution.py:31
  71.3 12.1 %fusion.23 = f32[128,2,32,512]{3,2,1,0:T(8,128)} fusion(bf16[2,128,64,32]{2,3,0,1:T(8,128)(2,1)S(1)} %copy-done.4, bf16[2,128,64,512]{3,2,1,0:T(8,128)(2,1)} %param.9), kind=kOutput, calls=%fused_computation.40 | convolution fusion | flops 536870912 | bytes 26214400 | tf_op jit(solution)/shard_map/bnkvu,kvm->bnkum/dot_general | solution.py:29
  83.4 12.9 %fusion.37 = bf16[2,1,128,32,512]{4,3,0,2,1:T(8,128)(2,1)} fusion(bf16[2,128,64,32]{2,3,0,1:T(8,128)(2,1)S(1)} %copy-done.2, bf16[2,128,64,512]{3,2,1,0:T(8,128)(2,1)} %param.9, f32[128,2,32,512]{3,2,1,0:T(8,128)} %fusion.23), kind=kOutput, calls=%fused_computation.83 | convolution fusion | flops 549453824 | bytes 34603008 | tf_op jit(solution)/shard_map/bnkvu,kvm->bnkum/dot_general | solution.py:30
  96.3 15.7 %copy.205 = bf16[2,1,128,32,512]{2,0,4,3,1:T(2,128)(2,1)} copy(bf16[2,1,128,32,512]{4,3,0,2,1:T(8,128)(2,1)} %fusion.37) | data formatting | bytes 16777216 | tf_op jit(solution)/shard_map/stack | solution.py:31
  112.0 26.4 %pad_maximum_fusion = bf16[2,2,1,128,16384]{3,1,2,0,4:T(2,128)(2,1)} fusion(bf16[1,2,1,128,16384]{3,1,2,0,4:T(2,128)(2,1)} %bitcast.343, bf16[1,2,1,128,16384]{3,1,2,0,4:T(2,128)(2,1)} %bitcast.342), kind=kLoop, calls=%fused_computation.3 | loop fusion | flops 8388608 | bytes 33554432 | tf_op jit(solution)/shard_map/stack | solution.py:31
  148.3 12.1 %slice_convert_fusion.1 = (f32[1,256,16,512]{3,2,1,0:T(8,128)}, f32[1,256,16,512]{3,2,1,0:T(8,128)}) fusion(bf16[2,256,16,512]{3,2,1,0:T(8,128)(2,1)} %param.11), kind=kLoop, calls=%fused_computation.91 | loop fusion | flops 4194304 | bytes 25165824 | tf_op jit(solution)/shard_map/convert_element_type | solution.py:73
  160.4 9.9 copy.203
  170.3 10.1 %copy.206 = f32[1,256,16,512]{1,3,2,0:T(8,128)} copy(f32[1,256,16,512]{3,2,1,0:T(8,128)} %get-tuple-element.18) | data formatting | bytes 16777216 | tf_op jit(solution)/shard_map/convert_element_type | solution.py:73
  180.4 150.8 %all-to-all-done = bf16[2,2,1,128,16384]{3,1,2,0,4:T(2,128)(2,1)} async-done(((bf16[2,2,1,128,16384]{3,1,2,0,4:T(2,128)(2,1)}), bf16[2,2,1,128,16384]{3,1,2,0,4:T(2,128)(2,1)}, u32[]{:S(2)}, u32[]{:S(2)}) %all-to-all-start) | async-done | bytes 16777248 | tf_op jit(solution)/shard_map/all_to_all | solution.py:66
  331.2 28.1 %copy.247 = bf16[2,2,1,128,2,8192]{3,4,5,1,2,0:T(2,128)(2,1)S(1)} copy(bf16[2,2,1,128,2,8192]{3,1,0,5,4,2:T(2,128)(2,1)} %bitcast.38) | data formatting | bytes 33554432 | tf_op jit(solution)/shard_map/all_to_all | solution.py:66
  359.2 13.0 %fusion.164 = (bf16[1,2,1,2,128,8192]{4,3,5,1,2,0:T(2,128)(2,1)}, bf16[1,2,1,2,128,8192]{4,3,5,1,2,0:T(2,128)(2,1)}) fusion(bf16[2,2,1,2,128,8192]{4,3,5,1,2,0:T(2,128)(2,1)S(1)} %bitcast.340), kind=kLoop, calls=%fused_computation.255 | loop fusion | bytes 33554432 | tf_op jit(solution)/shard_map/slice | solution.py:69
  372.3 14.1 %reshape.560 = bf16[2,256,8192]{1,2,0:T(8,128)(2,1)} reshape(bf16[1,2,1,2,128,8192]{4,3,5,1,2,0:T(2,128)(2,1)} %get-tuple-element.15) | data formatting | bytes 16777216 | tf_op jit(solution)/shard_map/reshape.30
  386.3 14.2 %reshape.559 = bf16[2,256,8192]{1,2,0:T(8,128)(2,1)} reshape(bf16[1,2,1,2,128,8192]{4,3,5,1,2,0:T(2,128)(2,1)} %get-tuple-element.16) | data formatting | bytes 16777216 | tf_op jit(solution)/shard_map/reshape.26
  400.6 12.6 %fusion.107 = f32[2,8192,256]{2,1,0:T(8,128)} fusion(bf16[2,256,8192]{1,2,0:T(8,128)(2,1)} %reshape.560, s32[256]{0:T(256)S(1)} %copy-done.6), kind=kOutput, calls=%fused_computation.180 | convolution fusion | flops 2148466688 | bytes 25166848 | tf_op jit(solution)/shard_map/fs,bnsc->bnfc/dot_general | solution.py:70
  422.2 14.8 %convolution_subtract_fusion = f32[2,8192,256]{2,1,0:T(8,128)} fusion(f32[2,8192,256]{2,1,0:T(8,128)} %fusion.107, bf16[2,256,8192]{1,2,0:T(8,128)(2,1)S(1)} %copy-done.1, s32[256]{0:T(256)S(1)} %copy-done.6), kind=kOutput, calls=%fused_computation.23 | convolution fusion | flops 2152660992 | bytes 41944064 | tf_op jit(solution)/shard_map/fs,bnsc->bnfc/dot_general | solution.py:72
  437.0 27.2 %fusion.11 = (bf16[2,256,8192]{1,2,0:T(8,128)(2,1)}, bf16[2,256,8192]{1,2,0:T(8,128)(2,1)}) fusion(f32[2,8192,256]{2,1,0:T(8,128)} %convolution_subtract_fusion, f32[256,8192]{0,1:T(8,128)} %bitcast.339, f32[256,8192]{0,1:T(8,128)} %bitcast.338, f32[2,8192,256]{2,1,0:T(8,128)} %fusion.109, bf16[2,256,8192]{1,2,0:T(8,128)(2,1)} %reshape.560, ...), kind=kOutput, calls=%fused_computation.28 | convolution fusion | flops 2186215424 | bytes 75498496 | tf_op jit(solution)/shard_map/fs,bnsc->bnfc/dot_general | solution.py:69
  464.2 12.6 %fusion.105 = f32[2,8192,256]{2,1,0:T(8,128)} fusion(bf16[2,256,8192]{1,2,0:T(8,128)(2,1)} %get-tuple-element.11, s32[256]{0:T(256)S(1)} %copy-done.6), kind=kOutput, calls=%fused_computation.179 | convolution fusion | flops 2148466688 | bytes 25166848 | tf_op jit(solution)/shard_map/fs,bnfc->bnsc/dot_general | solution.py:76
  485.8 13.7 %fusion.8 = bf16[1,2,1,256,8192]{3,4,1,2,0:T(8,128)(2,1)} fusion(f32[2,8192,256]{2,1,0:T(8,128)} %fusion.105, bf16[2,256,8192]{1,2,0:T(8,128)(2,1)} %get-tuple-element.12, s32[256]{0:T(256)S(1)} %copy-done.6), kind=kOutput, calls=%fused_computation.25 | convolution fusion | flops 2161049600 | bytes 33555456 | tf_op jit(solution)/shard_map/fs,bnfc->bnsc/dot_general | solution.py:77
  499.5 11.4 %fusion.9 = bf16[1,2,1,256,8192]{3,4,1,2,0:T(8,128)(2,1)} fusion(f32[2,8192,256]{2,1,0:T(8,128)} %fusion.103, bf16[2,256,8192]{1,2,0:T(8,128)(2,1)S(1)} %bitcast.337, s32[256]{0:T(256)S(1)} %copy-done.6), kind=kOutput, calls=%fused_computation.26 | convolution fusion | flops 2161049600 | bytes 33555456 | tf_op jit(solution)/shard_map/fs,bnfc->bnsc/dot_general | solution.py:81
  511.0 13.8 %pad_maximum_fusion.1 = bf16[2,2,1,256,8192]{3,4,1,2,0:T(8,128)(2,1)} fusion(bf16[1,2,1,256,8192]{3,4,1,2,0:T(8,128)(2,1)} %fusion.9, bf16[1,2,1,256,8192]{3,4,1,2,0:T(8,128)(2,1)} %fusion.8), kind=kLoop, calls=%fused_computation.4 | loop fusion | flops 8388608 | bytes 33554432 | tf_op jit(solution)/shard_map/stack | solution.py:84
  524.8 41.2 %copy.176 = bf16[2,2,1,256,8192]{4,1,2,0,3:T(2,128)(2,1)} copy(bf16[2,2,1,256,8192]{3,4,1,2,0:T(8,128)(2,1)} %pad_maximum_fusion.1) | data formatting | bytes 33554432 | tf_op jit(solution)/shard_map/stack | solution.py:84
  576.2 181.5 %all-to-all-done.1 = bf16[2,2,1,256,8192]{4,1,2,0,3:T(2,128)(2,1)} async-done(((bf16[2,2,1,256,8192]{4,1,2,0,3:T(2,128)(2,1)}), bf16[2,2,1,256,8192]{4,1,2,0,3:T(2,128)(2,1)}, u32[]{:S(2)}, u32[]{:S(2)}) %all-to-all-start.1) | async-done | bytes 16777248 | tf_op jit(solution)/shard_map/all_to_all | solution.py:83
  757.7 30.2 %copy.246 = bf16[2,2,1,2,128,8192]{5,3,1,4,2,0:T(2,128)(2,1)S(1)} copy(bf16[2,2,1,2,128,8192]{5,1,0,4,3,2:T(2,128)(2,1)} %bitcast.57) | data formatting | bytes 33554432 | tf_op jit(solution)/shard_map/all_to_all | solution.py:83
  787.9 14.9 %fusion.163 = (bf16[1,2,1,128,2,8192]{5,4,1,3,2,0:T(2,128)(2,1)}, bf16[1,2,1,128,2,8192]{5,4,1,3,2,0:T(2,128)(2,1)}) fusion(bf16[2,2,1,128,2,8192]{5,4,1,3,2,0:T(2,128)(2,1)S(1)} %bitcast.341), kind=kLoop, calls=%fused_computation.254 | loop fusion | bytes 33554432 | tf_op jit(solution)/shard_map/slice | solution.py:27
  802.8 14.3 %reshape.563 = bf16[2,128,32,512]{3,2,0,1:T(8,128)(2,1)} reshape(bf16[1,2,1,128,2,8192]{5,4,1,3,2,0:T(2,128)(2,1)} %get-tuple-element.13) | data formatting | bytes 16777216 | tf_op jit(solution)/shard_map/reshape.52
  817.1 14.3 %reshape.564 = bf16[2,128,32,512]{3,2,0,1:T(8,128)(2,1)} reshape(bf16[1,2,1,128,2,8192]{5,4,1,3,2,0:T(2,128)(2,1)} %get-tuple-element.14) | data formatting | bytes 16777216 | tf_op jit(solution)/shard_map/reshape.56
  831.3 10.2 %fusion.14 = f32[128,2,32,64]{3,2,1,0:T(8,128)} fusion(bf16[2,128,32,512]{3,2,0,1:T(8,128)(2,1)} %reshape.563, bf16[2,128,64,512]{3,2,1,0:T(8,128)(2,1)} %param.9), kind=kOutput, calls=%fused_computation.31 | convolution fusion | flops 536870912 | bytes 18874368 | tf_op jit(solution)/shard_map/bnkum,kvm->bnkvu/dot_general | solution.py:27
  854.1 10.2 %fusion.12 = f32[128,2,32,64]{3,2,1,0:T(8,128)} fusion(bf16[2,128,32,512]{3,2,0,1:T(8,128)(2,1)} %reshape.564, bf16[2,128,64,512]{3,2,1,0:T(8,128)(2,1)} %param.9), kind=kOutput, calls=%fused_computation.29 | convolution fusion | flops 536870912 | bytes 18874368 | tf_op jit(solution)/shard_map/bnkum,kvm->bnkvu/dot_general | solution.py:30
  864.3 10.7 %fusion.47 = bf16[2,1,128,64,32]{3,4,0,2,1:T(8,128)(2,1)} fusion(f32[128,2,32,64]{3,2,1,0:T(8,128)} %fusion.12, bf16[2,128,32,512]{3,2,0,1:T(8,128)(2,1)} %reshape.563, bf16[2,128,64,512]{3,2,1,0:T(8,128)(2,1)} %param.9), kind=kOutput, calls=%fused_computation.99 | convolution fusion | flops 537919488 | bytes 22020096 | tf_op jit(solution)/shard_map/bnkum,kvm->bnkvu/dot_general | solution.py:29
  900.8 13.5 %collective-permute-done.4 = bf16[1,2,2,1,128,4,32]{4,6,5,0,3,2,1:T(8,128)(2,1)S(1)} collective-permute-done((bf16[1,2,2,1,128,4,32]{4,6,5,0,3,2,1:T(8,128)(2,1)S(1)}, bf16[1,2,2,1,128,4,32]{4,6,5,0,3,2,1:T(8,128)(2,1)S(1)}, u32[]{:S(2)}, u32[]{:S(2)}) %collective-permute-start.4) | collective-permute-done | bytes 131104 | tf_op jit(solution)/shard_map/ppermute | solution.py:100
  971.1 12.3 %collective-permute-done.15 = bf16[2,2,1,128,4,128]{5,3,4,2,1,0:T(8,128)(2,1)S(1)} collective-permute-done((bf16[2,2,1,128,4,128]{5,3,4,2,1,0:T(8,128)(2,1)S(1)}, bf16[2,2,1,128,4,128]{5,3,4,2,1,0:T(8,128)(2,1)S(1)}, u32[]{:S(2)}, u32[]{:S(2)}) %collective-permute-start.15) | collective-permute-done | bytes 524320 | tf_op jit(solution)/shard_map/ppermute | solution.py:23
  (122 shorter events, 173.5 us)
Async XLA Ops:
  6.5 932.5 %all-gather.2.cloned.1.call-start = ((), (), s32[]{:S(2)}) async-start(), calls=%async_computation.2 | async-start | bytes 35651584 | tf_op jit(solution)/shard_map/all_gather | solution.py:106
  16.0 14.9 %slice-start = ((s8[16777216]{0:T(1024)(128)(4,1)}), s8[4194304]{0:T(1024)(128)(4,1)S(1)}, s32[]{:S(2)}) async-start(s8[16777216]{0:T(1024)(128)(4,1)} %bitcast.334), calls=%async_computation.3 | async-start | bytes 8388608
  16.0 14.9 %slice-start.1 = ((s8[16777216]{0:T(1024)(128)(4,1)}), s8[4194304]{0:T(1024)(128)(4,1)S(1)}, s32[]{:S(2)}) async-start(s8[16777216]{0:T(1024)(128)(4,1)} %bitcast.334), calls=%async_computation.4 | async-start | bytes 8388608
  20.0 10.9 %slice-start.2 = ((s8[16777216]{0:T(1024)(128)(4,1)}), s8[4194304]{0:T(1024)(128)(4,1)S(1)}, s32[]{:S(2)}) async-start(s8[16777216]{0:T(1024)(128)(4,1)} %bitcast.334), calls=%async_computation.5 | async-start | bytes 8388608
  54.8 16.5 %copy-start.4 = (bf16[2,128,64,32]{2,3,0,1:T(8,128)(2,1)S(1)}, bf16[2,128,64,32]{2,3,0,1:T(8,128)(2,1)}, u32[]{:S(2)}) copy-start(bf16[2,128,64,32]{2,3,0,1:T(8,128)(2,1)} %fusion.44) | copy-start | bytes 3145732
  71.3 12.1 %copy-start.2 = (bf16[2,128,64,32]{2,3,0,1:T(8,128)(2,1)S(1)}, bf16[2,128,64,32]{2,3,0,1:T(8,128)(2,1)}, u32[]{:S(2)}) copy-start(bf16[2,128,64,32]{2,3,0,1:T(8,128)(2,1)} %fusion.45) | copy-start | bytes 3145732
  138.4 192.7 %all-to-all-start = ((bf16[2,2,1,128,16384]{3,1,2,0,4:T(2,128)(2,1)}), bf16[2,2,1,128,16384]{3,1,2,0,4:T(2,128)(2,1)}, u32[]{:S(2)}, u32[]{:S(2)}) async-start(bf16[2,2,1,128,16384]{3,1,2,0,4:T(2,128)(2,1)} %pad_maximum_fusion), calls=%async_computation | async-start | bytes 33554432 | tf_op jit(solution)/shard_map/all_to_all | solution.py:66
  386.3 14.2 %copy-start.6 = (s32[256]{0:T(256)S(1)}, s32[256]{0:T(256)}, u32[]{:S(2)}) copy-start(s32[256]{0:T(256)} %param.14) | copy-start | bytes 3076
  400.5 12.6 %copy-start.1 = (bf16[2,256,8192]{1,2,0:T(8,128)(2,1)S(1)}, bf16[2,256,8192]{1,2,0:T(8,128)(2,1)}, u32[]{:S(2)}) copy-start(bf16[2,256,8192]{1,2,0:T(8,128)(2,1)} %reshape.559) | copy-start | bytes 25165828
  464.2 12.6 %copy-start = (bf16[2,256,8192]{1,2,0:T(8,128)(2,1)S(1)}, bf16[2,256,8192]{1,2,0:T(8,128)(2,1)}, u32[]{:S(2)}) copy-start(bf16[2,256,8192]{1,2,0:T(8,128)(2,1)} %get-tuple-element.12) | copy-start | bytes 25165828
  464.2 35.3 %slice-start.4 = ((s8[8388608]{0:T(1024)(128)(4,1)}), s8[4194304]{0:T(1024)(128)(4,1)S(1)}, s32[]{:S(2)}) async-start(s8[8388608]{0:T(1024)(128)(4,1)} %bitcast.336), calls=%async_computation.7 | async-start | bytes 8388608
  476.8 22.7 %slice-start.5 = ((s8[8388608]{0:T(1024)(128)(4,1)}), s8[4194304]{0:T(1024)(128)(4,1)S(1)}, s32[]{:S(2)}) async-start(s8[8388608]{0:T(1024)(128)(4,1)} %bitcast.336), calls=%async_computation.8 | async-start | bytes 8388608
  565.9 191.8 %all-to-all-start.1 = ((bf16[2,2,1,256,8192]{4,1,2,0,3:T(2,128)(2,1)}), bf16[2,2,1,256,8192]{4,1,2,0,3:T(2,128)(2,1)}, u32[]{:S(2)}, u32[]{:S(2)}) async-start(bf16[2,2,1,256,8192]{4,1,2,0,3:T(2,128)(2,1)} %copy.176), calls=%async_computation.1 | async-start | bytes 33554432 | tf_op jit(solution)/shard_map/all_to_all | solution.py:83
  879.5 50.7 %collective-permute-start.10 = (bf16[1,2,2,1,128,4,32]{4,6,5,0,3,2,1:T(8,128)(2,1)S(1)}, bf16[1,2,2,1,128,4,32]{4,6,5,0,3,2,1:T(8,128)(2,1)S(1)}, u32[]{:S(2)}, u32[]{:S(2)}) collective-permute-start(bf16[1,2,2,1,128,4,32]{4,6,5,0,3,2,1:T(8,128)(2,1)S(1)} %get-tuple-element.39), channel_id=1, source_target_pairs={{0,11},{1,12},{2,13},{3,14},{4,15},{5,0},{6,1},{7,2},{8,3},{9,4},{... | collective-permute-start | bytes 393224 | tf_op jit(solution)/shard_map/ppermute | solution.py:100
  880.7 8.5 collective-permute-start
  883.4 9.2 collective-permute-start.1
  884.4 29.9 %collective-permute-start.5 = (bf16[1,2,2,1,128,4,32]{4,6,5,0,3,2,1:T(8,128)(2,1)S(1)}, bf16[1,2,2,1,128,4,32]{4,6,5,0,3,2,1:T(8,128)(2,1)S(1)}, u32[]{:S(2)}, u32[]{:S(2)}) collective-permute-start(bf16[1,2,2,1,128,4,32]{4,6,5,0,3,2,1:T(8,128)(2,1)S(1)} %get-tuple-element.33), channel_id=1, source_target_pairs={{0,6},{1,7},{2,8},{3,9},{4,10},{5,11},{6,12},{7,13},{8,14},{9,15},... | collective-permute-start | bytes 393224 | tf_op jit(solution)/shard_map/ppermute | solution.py:100
  884.7 11.5 %collective-permute-start.2 = (bf16[1,2,2,1,128,4,32]{4,6,5,0,3,2,1:T(8,128)(2,1)S(1)}, bf16[1,2,2,1,128,4,32]{4,6,5,0,3,2,1:T(8,128)(2,1)S(1)}, u32[]{:S(2)}, u32[]{:S(2)}) collective-permute-start(bf16[1,2,2,1,128,4,32]{4,6,5,0,3,2,1:T(8,128)(2,1)S(1)} %get-tuple-element.29), channel_id=1, source_target_pairs={{0,3},{1,4},{2,5},{3,6},{4,7},{5,8},{6,9},{7,10},{8,11},{9,12},{10... | collective-permute-start | bytes 393224 | tf_op jit(solution)/shard_map/ppermute | solution.py:100
  889.1 11.6 %collective-permute-start.3 = (bf16[1,2,2,1,128,4,32]{4,6,5,0,3,2,1:T(8,128)(2,1)S(1)}, bf16[1,2,2,1,128,4,32]{4,6,5,0,3,2,1:T(8,128)(2,1)S(1)}, u32[]{:S(2)}, u32[]{:S(2)}) collective-permute-start(bf16[1,2,2,1,128,4,32]{4,6,5,0,3,2,1:T(8,128)(2,1)S(1)} %get-tuple-element.30), channel_id=1, source_target_pairs={{0,4},{1,5},{2,6},{3,7},{4,8},{5,9},{6,10},{7,11},{8,12},{9,13},{1... | collective-permute-start | bytes 393224 | tf_op jit(solution)/shard_map/ppermute | solution.py:100
  892.6 21.7 %collective-permute-start.4 = (bf16[1,2,2,1,128,4,32]{4,6,5,0,3,2,1:T(8,128)(2,1)S(1)}, bf16[1,2,2,1,128,4,32]{4,6,5,0,3,2,1:T(8,128)(2,1)S(1)}, u32[]{:S(2)}, u32[]{:S(2)}) collective-permute-start(bf16[1,2,2,1,128,4,32]{4,6,5,0,3,2,1:T(8,128)(2,1)S(1)} %get-tuple-element.31), channel_id=1, source_target_pairs={{0,5},{1,6},{2,7},{3,8},{4,9},{5,10},{6,11},{7,12},{8,13},{9,14},{... | collective-permute-start | bytes 393224 | tf_op jit(solution)/shard_map/ppermute | solution.py:100
  896.2 18.2 %collective-permute-start.6 = (bf16[1,2,2,1,128,4,32]{4,6,5,0,3,2,1:T(8,128)(2,1)S(1)}, bf16[1,2,2,1,128,4,32]{4,6,5,0,3,2,1:T(8,128)(2,1)S(1)}, u32[]{:S(2)}, u32[]{:S(2)}) collective-permute-start(bf16[1,2,2,1,128,4,32]{4,6,5,0,3,2,1:T(8,128)(2,1)S(1)} %get-tuple-element.34), channel_id=1, source_target_pairs={{0,7},{1,8},{2,9},{3,10},{4,11},{5,12},{6,13},{7,14},{8,15},{9,0},... | collective-permute-start | bytes 393224 | tf_op jit(solution)/shard_map/ppermute | solution.py:100
  900.7 14.5 %collective-permute-start.7 = (bf16[1,2,2,1,128,4,32]{4,6,5,0,3,2,1:T(8,128)(2,1)S(1)}, bf16[1,2,2,1,128,4,32]{4,6,5,0,3,2,1:T(8,128)(2,1)S(1)}, u32[]{:S(2)}, u32[]{:S(2)}) collective-permute-start(bf16[1,2,2,1,128,4,32]{4,6,5,0,3,2,1:T(8,128)(2,1)S(1)} %get-tuple-element.35), channel_id=1, source_target_pairs={{0,8},{1,9},{2,10},{3,11},{4,12},{5,13},{6,14},{7,15},{8,0},{9,1},... | collective-permute-start | bytes 393224 | tf_op jit(solution)/shard_map/ppermute | solution.py:100
  914.3 9.9 collective-permute-start.8
  914.3 13.8 %collective-permute-start.9 = (bf16[1,2,2,1,128,4,32]{4,6,5,0,3,2,1:T(8,128)(2,1)S(1)}, bf16[1,2,2,1,128,4,32]{4,6,5,0,3,2,1:T(8,128)(2,1)S(1)}, u32[]{:S(2)}, u32[]{:S(2)}) collective-permute-start(bf16[1,2,2,1,128,4,32]{4,6,5,0,3,2,1:T(8,128)(2,1)S(1)} %get-tuple-element.37), channel_id=1, source_target_pairs={{0,10},{1,11},{2,12},{3,13},{4,14},{5,15},{6,0},{7,1},{8,2},{9,3},... | collective-permute-start | bytes 393224 | tf_op jit(solution)/shard_map/ppermute | solution.py:100
  914.4 15.8 %collective-permute-start.11 = (bf16[1,2,2,1,128,4,32]{4,6,5,0,3,2,1:T(8,128)(2,1)S(1)}, bf16[1,2,2,1,128,4,32]{4,6,5,0,3,2,1:T(8,128)(2,1)S(1)}, u32[]{:S(2)}, u32[]{:S(2)}) collective-permute-start(bf16[1,2,2,1,128,4,32]{4,6,5,0,3,2,1:T(8,128)(2,1)S(1)} %get-tuple-element.40), channel_id=1, source_target_pairs={{0,12},{1,13},{2,14},{3,15},{4,0},{5,1},{6,2},{7,3},{8,4},{9,5},{1... | collective-permute-start | bytes 393224 | tf_op jit(solution)/shard_map/ppermute | solution.py:100
  915.2 15.1 %collective-permute-start.12 = (bf16[1,2,2,1,128,4,32]{4,6,5,0,3,2,1:T(8,128)(2,1)S(1)}, bf16[1,2,2,1,128,4,32]{4,6,5,0,3,2,1:T(8,128)(2,1)S(1)}, u32[]{:S(2)}, u32[]{:S(2)}) collective-permute-start(bf16[1,2,2,1,128,4,32]{4,6,5,0,3,2,1:T(8,128)(2,1)S(1)} %get-tuple-element.38), channel_id=1, source_target_pairs={{0,13},{1,14},{2,15},{3,0},{4,1},{5,2},{6,3},{7,4},{8,5},{9,6},{10... | collective-permute-start | bytes 393224 | tf_op jit(solution)/shard_map/ppermute | solution.py:100
  924.2 9.5 collective-permute-start.13
  928.2 6.0 collective-permute-start.14
  960.3 9.2 copy-start.8
  967.3 18.6 %copy-start.5 = (f32[128,128]{1,0:T(8,128)S(1)}, f32[128,128]{1,0:T(8,128)}, u32[]{:S(2)}) copy-start(f32[128,128]{1,0:T(8,128)} %param.13) | copy-start | bytes 196612
  967.4 18.6 %copy-start.7 = (f32[128,4]{0,1:T(4,128)S(1)}, f32[128,4]{0,1:T(4,128)}, u32[]{:S(2)}) copy-start(f32[128,4]{0,1:T(4,128)} %param.12) | copy-start | bytes 6148
  968.8 14.6 %collective-permute-start.15 = (bf16[2,2,1,128,4,128]{5,3,4,2,1,0:T(8,128)(2,1)S(1)}, bf16[2,2,1,128,4,128]{5,3,4,2,1,0:T(8,128)(2,1)S(1)}, u32[]{:S(2)}, u32[]{:S(2)}) collective-permute-start(bf16[2,2,1,128,4,128]{5,3,4,2,1,0:T(8,128)(2,1)S(1)} %pad_maximum_fusion.4), channel_id=1, source_target_pairs={{0,16},{16,0},{1,17},{17,1},{2,18},{18,2},{3,19},{19,3},{4,20},{20... | collective-permute-start | bytes 1572872 | tf_op jit(solution)/shard_map/ppermute | solution.py:23
  (2 other events, 10.0 us)
Sparse Core Ops, SparseCore 0:
  8.9 170.7 all-gather.1
